TPU v7x, 256 devices: a whole 4x4x8 slice. The times are simulated.
256 devices in a mesh: snap: 16 (over z, core), vert: 16 (over y, x).
Axes of the slice: x: 4, y: 4, z: 8, core: 2. Of those that a mesh axis runs over, the one named last changes fastest.
Arguments:
- saved_gates: bfloat16 [16, 8192, 1536], P(None, ('vert', 'snap')), may hold values from -1 to 1, as said below
- saved_cells: bfloat16 [16, 8192, 384], P(None, ('vert', 'snap')), may hold values from -4 to 4
- conv_out: float32 [16, 8192, 384], P(None, ('vert', 'snap')), may hold values from -6 to 6
- out_grad: float32 [16, 8192, 384], P(None, ('vert', 'snap')), may hold values from -6 to 6
- input_weight: float32 [384, 1536], replicated, may hold values from -0.3125 to 0.3125
- recur_weight: float32 [384, 1536], replicated, may hold values from -0.3125 to 0.3125
- conv_weight: float32 [384, 384], replicated, may hold values from -0.3125 to 0.3125
- node_feats: float32 [16, 8192, 384], P('snap', 'vert'), may hold values from -6 to 6
- tile_values: bfloat16 [16, 16, 5, 512, 512], P('snap', 'vert'), may hold values from -0.15625 to 0.15625
- tile_mask: int32 [16, 16, 5], P('snap', 'vert'), may hold values 0 or 1
Outputs:
- feat_grad: float32 [16, 8192, 384], P('snap', 'vert')
- conv_weight_grad: float32 [147456], P(('snap', 'vert'))
- input_weight_grad: float32 [589824], P(('snap', 'vert'))
- recur_weight_grad: float32 [589824], P(('snap', 'vert'))
Inputs may be any that keep to these rules, and one draw needn't show every extreme that they name: `saved_gates`: the first and fourth blocks of 384 entries lie strictly between 0 and 1, the second in (0, 1], the third strictly between -1 and 1.
All inputs are finite; a program needn't handle non-finite values. No bound on the sum of `tile_mask` on one device may be relied on, other than what follows from the above.
Results may differ from a plain program's by a relative error of at most 0.0029.
Values may be sent and summed in bfloat16 or wider, within the bound.
A program may use at most 128 MiB of HBM per device.

v0:
```python
import jax
import jax.numpy as jnp
from jax import lax
from jax.sharding import PartitionSpec as P


def passed_along(shard, axis, by):
    size = lax.axis_size(axis)
    pairs = [(i, i + by) for i in range(size) if 0 <= i + by < size]
    return lax.ppermute(shard, axis, pairs)


def cell_backward(saved_gates, saved_cells, out_grad, recur_weight):
    feat_width = saved_cells.shape[-1]
    gate_vals = saved_gates.astype(jnp.float32)
    cell_vals = saved_cells.astype(jnp.float32)
    prev_cells = jnp.concatenate([jnp.zeros_like(cell_vals[:1]), cell_vals[:-1]], axis=0)

    def reverse_step(carry, inputs):
        rec_grad, cell_grad = carry
        gate_now, cell_now, cell_before, grad_now = inputs
        in_gate = gate_now[:, :feat_width]
        forget = gate_now[:, feat_width : 2 * feat_width]
        candidate = gate_now[:, 2 * feat_width : 3 * feat_width]
        out_gate = gate_now[:, 3 * feat_width :]
        total_grad = grad_now + rec_grad
        squashed = jnp.tanh(cell_now)
        cell_total = cell_grad + total_grad * out_gate * (1.0 - squashed * squashed)
        pre_grad = jnp.concatenate(
            [
                cell_total * candidate * in_gate * (1.0 - in_gate),
                cell_total * cell_before * forget * (1.0 - forget),
                cell_total * in_gate * (1.0 - candidate * candidate),
                total_grad * squashed * out_gate * (1.0 - out_gate),
            ],
            axis=-1,
        )
        new_rec = jnp.dot(
            pre_grad,
            recur_weight.T,
            precision=lax.Precision.HIGHEST,
            preferred_element_type=jnp.float32,
        )
        return ((new_rec, cell_total * forget), pre_grad)

    row_total = cell_vals.shape[1]
    begin = (
        jnp.zeros((row_total, feat_width), jnp.float32),
        jnp.zeros((row_total, feat_width), jnp.float32),
    )
    unused, pre_grads = lax.scan(
        reverse_step, begin, (gate_vals, cell_vals, prev_cells, out_grad), reverse=True
    )
    last_out = gate_vals[:, :, 3 * feat_width :]
    prev_out = jnp.concatenate([jnp.zeros_like(last_out[:1]), last_out[:-1]], axis=0)
    prev_hidden = prev_out * jnp.tanh(prev_cells)
    return (pre_grads, prev_hidden)


def pass_direct(piece, offset):
    return passed_along(piece, "vert", offset)


def local(
    saved_gates,
    saved_cells,
    conv_out,
    out_grad,
    input_weight,
    recur_weight,
    conv_weight,
    node_feats,
    tile_values,
    tile_mask,
):
    pre_grads, prev_hidden = cell_backward(saved_gates, saved_cells, out_grad, recur_weight)
    conv_in_grad = jnp.einsum(
        "tvg,fg->tvf",
        pre_grads,
        input_weight,
        precision=lax.Precision.HIGHEST,
        preferred_element_type=jnp.float32,
    )
    input_term = jnp.einsum(
        "tvf,tvg->fg",
        conv_out,
        pre_grads,
        precision=lax.Precision.HIGHEST,
        preferred_element_type=jnp.float32,
    ).reshape(-1)
    recur_term = jnp.einsum(
        "tvf,tvg->fg",
        prev_hidden,
        pre_grads,
        precision=lax.Precision.HIGHEST,
        preferred_element_type=jnp.float32,
    ).reshape(-1)
    input_weight_grad, recur_weight_grad = (
        lax.psum_scatter(input_term, ("snap", "vert"), scatter_dimension=0, tiled=True),
        lax.psum_scatter(recur_term, ("snap", "vert"), scatter_dimension=0, tiled=True),
    )
    rounded = lax.all_to_all(
        conv_in_grad.astype(jnp.bfloat16), "snap", split_axis=0, concat_axis=1, tiled=True
    )
    tiles = tile_values[:, 0]
    partial_value = jnp.einsum("skij,sif->skjf", tiles, rounded, preferred_element_type=jnp.float32)
    slot_count = tiles.shape[1]
    reach_blocks = (slot_count - 1) // 2
    position = lax.axis_index("vert")
    block_count = lax.axis_size("vert")
    target = position + jnp.arange(slot_count, dtype=jnp.int32) - reach_blocks
    inside = (target >= 0) & (target < block_count)
    present = (tile_mask[:, 0, :] == 1) & inside[None, :]
    partial_value = partial_value * present.astype(jnp.float32)[:, :, None, None]
    z_grad = partial_value[:, reach_blocks]
    for slot in range(slot_count):
        offset = slot - reach_blocks
        if offset != 0:
            z_grad = z_grad + pass_direct(partial_value[:, slot], offset)
    feat_grad = jnp.einsum(
        "sbg,fg->sbf",
        z_grad,
        conv_weight,
        precision=lax.Precision.HIGHEST,
        preferred_element_type=jnp.float32,
    )
    conv_term = jnp.einsum(
        "sbf,sbg->fg",
        node_feats,
        z_grad,
        precision=lax.Precision.HIGHEST,
        preferred_element_type=jnp.float32,
    ).reshape(-1)
    conv_weight_grad = lax.psum_scatter(
        conv_term, ("snap", "vert"), scatter_dimension=0, tiled=True
    )
    return (feat_grad, conv_weight_grad, input_weight_grad, recur_weight_grad)


def solution(mesh):
    placed = (
        P(None, ("vert", "snap"), None),
        P(None, ("vert", "snap"), None),
        P(None, ("vert", "snap"), None),
        P(None, ("vert", "snap"), None),
        P(),
        P(),
        P(),
        P("snap", "vert", None),
        P("snap", "vert", None, None, None),
        P("snap", "vert", None),
    )
    return jax.shard_map(
        local,
        mesh=mesh,
        in_specs=placed,
        out_specs=(
            P("snap", "vert", None),
            P(("snap", "vert")),
            P(("snap", "vert")),
            P(("snap", "vert")),
        ),
        check_vma=False,
    )
```

profile of v0, /device:TPU:8, one launch (start us, length us, event | category | flops | bytes accessed | tf_op | source)
XLA Modules:
  0.0 538.3 jit_solution(3331778018956491245)
XLA Ops:
  7.2 1.2 slice.74
  8.4 2.0 convert_element_type.19
  10.4 3.5 convert_element_type.18
  14.8 2.1 broadcast_in_dim.15
  17.5 135.6 %while.19 = (s32[]{:T(128)}, f32[32,384]{1,0:T(8,128)}, f32[32,384]{1,0:T(8,128)}, f32[16,32,1536]{2,1,0:T(8,128)}, f32[16,32,384]{2,1,0:T(8,128)}, /*index=5*/f...) while((s32[]{:T(128)}, f32[32,384]{1,0:T(8,128)}, ...), condition=%wide.region_1.2_spmd.clone, body=%wide.region_0.1_spmd.clone.sunk | while | flops 227082240 | bytes 4227227 | solution.py:51
  18.4 1.5 slice_multiply_fusion.2
  21.5 4.5 fusion.44
  26.9 1.5 slice_multiply_fusion.2
  29.9 4.5 fusion.44
  35.4 1.5 slice_multiply_fusion.2
  38.4 4.5 fusion.44
  43.8 1.5 slice_multiply_fusion.2
  46.9 4.5 fusion.44
  52.3 1.5 slice_multiply_fusion.2
  55.3 4.5 fusion.44
  60.8 1.5 slice_multiply_fusion.2
  63.8 4.5 fusion.44
  69.2 1.5 slice_multiply_fusion.2
  72.3 4.5 fusion.44
  77.7 1.5 slice_multiply_fusion.2
  80.8 4.5 fusion.44
  86.2 1.5 slice_multiply_fusion.2
  89.3 4.5 fusion.44
  94.7 1.5 slice_multiply_fusion.2
  97.8 4.5 fusion.44
  103.2 1.5 slice_multiply_fusion.2
  106.2 4.5 fusion.44
  111.7 1.5 slice_multiply_fusion.2
  114.7 4.5 fusion.44
  120.2 1.5 slice_multiply_fusion.2
  123.2 4.5 fusion.44
  128.6 1.5 slice_multiply_fusion.2
  131.7 4.5 fusion.44
  137.1 1.5 slice_multiply_fusion.2
  140.2 4.5 fusion.44
  145.6 1.5 slice_multiply_fusion.2
  148.6 4.5 fusion.44
  153.1 8.5 %fusion.15 = bf16[16,32,384]{2,1,0:T(8,128)(2,1)} fusion(f32[16,32,1536]{2,1,0:T(8,128)} %get-tuple-element.183, f32[384,1536]{1,0:T(8,128)} %param.16), kind=kOutput, calls=%fused_computation.28 | convolution fusion | flops 3624075264 | bytes 5898240 | tf_op jit(solution)/shard_map/tvg,fg->tvf/dot_general | solution.py:77
  161.6 8.6 %all-to-all-start = ((bf16[16,32,384]{2,1,0:T(8,128)(2,1)}), bf16[16,32,384]{2,1,0:T(8,128)(2,1)}, u32[]{:S(2)}, u32[]{:S(2)}) async-start(bf16[16,32,384]{2,1,0:T(8,128)(2,1)} %fusion.15), calls=%async_computation | async-start | bytes 786432 | tf_op jit(solution)/shard_map/all_to_all | solution.py:102
  170.3 1.9 slice.80
  172.2 11.8 %all-to-all-done = bf16[16,32,384]{2,1,0:T(8,128)(2,1)} async-done(((bf16[16,32,384]{2,1,0:T(8,128)(2,1)}), bf16[16,32,384]{2,1,0:T(8,128)(2,1)}, u32[]{:S(2)}, u32[]{:S(2)}) %all-to-all-start) | async-done | bytes 393248 | tf_op jit(solution)/shard_map/all_to_all | solution.py:102
  184.0 2.2 multiply_bitcast_fusion
  186.2 1.7 slice_bitcast_fusion.3
  187.9 1.8 copy-done.1
  189.7 4.9 collective-permute-start
  194.6 3.1 collective-permute-start.1
  197.7 2.8 collective-permute-start.2
  200.5 2.6 collective-permute-start.3
  203.1 5.4 %convolution_bitcast_fusion = f32[384,1536]{1,0:T(8,128)} fusion(f32[16,32,1536]{2,1,0:T(8,128)S(1)} %copy-done.2, f32[15,32,384]{2,1,0:T(8,128)S(1)} %copy-done.4, f32[15,32,384]{2,1,0:T(8,128)S(1)} %slice.74), kind=kOutput, calls=%fused_computation.21 | convolution fusion | flops 3624075264 | bytes 6979584 | tf_op jit(solution)/shard_map/tvf,tvg->fg/dot_general | solution.py:91
  208.6 3.2 reshape.70
  211.8 7.7 %convolution_bitcast_fusion.1 = f32[384,1536]{0,1:T(8,128)} fusion(f32[16,32,1536]{2,1,0:T(8,128)} %get-tuple-element.183, f32[16,32,384]{2,1,0:T(8,128)S(1)} %copy-done.5), kind=kOutput, calls=%fused_computation.22 | convolution fusion | flops 3623878656 | bytes 6291456 | tf_op jit(solution)/shard_map/tvf,tvg->fg/dot_general | solution.py:84
  219.5 3.1 copy.20
  222.6 3.1 reshape.69
  225.8 4.8 collective-permute-done.1
  230.9 16.3 %collective-permute-done.3 = f32[1,512,384]{1,2,0:T(8,128)} collective-permute-done((f32[1,512,384]{1,2,0:T(8,128)}, f32[1,512,384]{1,2,0:T(8,128)}, u32[]{:S(2)}, u32[]{:S(2)}) %collective-permute-start.3) | collective-permute-done | bytes 786464 | tf_op jit(solution)/shard_map/ppermute | solution.py:10
  247.3 2.5 fusion.22
  249.8 2.2 convolution_bitcast_fusion.3
  252.0 2.1 copy.19
  254.2 1.9 reshape.68
  256.1 4.6 convolution_bitcast_fusion.2
  260.7 266.6 %all-reduce.8.cloned.1.call-done = (f32[147456]{0:T(1024)}, f32[589824]{0:T(1024)}, f32[589824]{0:T(1024)}) async-done(((f32[147456]{0:T(1024)}, f32[589824]{0:T(1024)}, f32[589824]{0:T(1024)}), (f32[147456]{0:T(1024)}, f32[589824]{0:T(1024)}, f32[589824]{0:T(1024)})) %all-reduce.8.cloned.1.call-update) | async-done | bytes 5308432
  527.3 1.4 dynamic-slice.1
  528.7 1.4 dynamic-slice.2
  530.1 1.4 dynamic-slice
  (69 shorter events, 41.5 us)
Async XLA Ops:
  7.2 176.8 %copy-start = (bf16[1,1,5,512,512]{4,3,2,1,0:T(8,128)(2,1)S(1)}, bf16[1,1,5,512,512]{4,3,2,1,0:T(8,128)(2,1)}, u32[]{:S(2)}) copy-start(bf16[1,1,5,512,512]{4,3,2,1,0:T(8,128)(2,1)} %param.20) | copy-start | bytes 7864324
  153.1 19.1 %copy-start.6 = (s32[1,1,5]{2,1,0:T(1,128)S(1)}, s32[1,1,5]{2,1,0:T(1,128)}, u32[]{:S(2)}) copy-start(s32[1,1,5]{2,1,0:T(1,128)} %param.21) | copy-start | bytes 64
  161.6 22.4 %all-to-all-start = ((bf16[16,32,384]{2,1,0:T(8,128)(2,1)}), bf16[16,32,384]{2,1,0:T(8,128)(2,1)}, u32[]{:S(2)}, u32[]{:S(2)}) async-start(bf16[16,32,384]{2,1,0:T(8,128)(2,1)} %fusion.15), calls=%async_computation | async-start | bytes 786432 | tf_op jit(solution)/shard_map/all_to_all | solution.py:102
  170.2 357.1 %all-reduce.8.cloned.1.call-start = ((), (), s32[]{:S(2)}) async-start(), calls=%async_computation.1 | async-start | bytes 10616832
  186.2 3.5 copy-start.1
  186.2 16.9 %copy-start.2 = (f32[16,32,1536]{2,1,0:T(8,128)S(1)}, f32[16,32,1536]{2,1,0:T(8,128)}, u32[]{:S(2)}) copy-start(f32[16,32,1536]{2,1,0:T(8,128)} %get-tuple-element.183) | copy-start | bytes 9437188
  186.2 16.9 %copy-start.4 = (f32[15,32,384]{2,1,0:T(8,128)S(1)}, f32[15,32,384]{2,1,0:T(8,128)}, u32[]{:S(2)}) copy-start(f32[15,32,384]{2,1,0:T(8,128)} %slice.80) | copy-start | bytes 2211844
  189.7 36.1 %collective-permute-start = (f32[1,512,384]{1,2,0:T(8,128)}, f32[1,512,384]{1,2,0:T(8,128)}, u32[]{:S(2)}, u32[]{:S(2)}) collective-permute-start(f32[1,512,384]{1,2,0:T(8,128)} %get-tuple-element.241), channel_id=1, source_target_pairs={{2,0},{3,1},{4,2},{5,3},{6,4},{7,5},{8,6},{9,7},{10,8},{11,9},{12,... | collective-permute-start | bytes 2359304 | tf_op jit(solution)/shard_map/ppermute | solution.py:10
  194.6 35.9 %collective-permute-start.1 = (f32[1,512,384]{1,2,0:T(8,128)}, f32[1,512,384]{1,2,0:T(8,128)}, u32[]{:S(2)}, u32[]{:S(2)}) collective-permute-start(f32[1,512,384]{1,2,0:T(8,128)} %get-tuple-element.244), channel_id=1, source_target_pairs={{1,0},{2,1},{3,2},{4,3},{5,4},{6,5},{7,6},{8,7},{9,8},{10,9},{11,1... | collective-permute-start | bytes 2359304 | tf_op jit(solution)/shard_map/ppermute | solution.py:10
  197.7 33.2 %collective-permute-start.2 = (f32[1,512,384]{1,2,0:T(8,128)}, f32[1,512,384]{1,2,0:T(8,128)}, u32[]{:S(2)}, u32[]{:S(2)}) collective-permute-start(f32[1,512,384]{1,2,0:T(8,128)} %get-tuple-element.243), channel_id=1, source_target_pairs={{0,1},{1,2},{2,3},{3,4},{4,5},{5,6},{6,7},{7,8},{8,9},{9,10},{10,1... | collective-permute-start | bytes 2359304 | tf_op jit(solution)/shard_map/ppermute | solution.py:10
  200.5 46.8 %collective-permute-start.3 = (f32[1,512,384]{1,2,0:T(8,128)}, f32[1,512,384]{1,2,0:T(8,128)}, u32[]{:S(2)}, u32[]{:S(2)}) collective-permute-start(f32[1,512,384]{1,2,0:T(8,128)} %get-tuple-element.242), channel_id=1, source_target_pairs={{0,2},{1,3},{2,4},{3,5},{4,6},{5,7},{6,8},{7,9},{8,10},{9,11},{10,... | collective-permute-start | bytes 2359304 | tf_op jit(solution)/shard_map/ppermute | solution.py:10
  208.6 3.2 copy-start.5
  225.8 24.1 %copy-start.3 = (f32[1,512,384]{2,1,0:T(8,128)S(1)}, f32[1,512,384]{2,1,0:T(8,128)}, u32[]{:S(2)}) copy-start(f32[1,512,384]{2,1,0:T(8,128)} %param.19) | copy-start | bytes 2359300
Sparse Core Ops, SparseCore 0:
  256.2 271.0 all-reduce.7
where the time goes:
time: 542 us; the launch traced here: 538 us
  waiting for transfers between devices  300 us (55%)
  matrix products  102 us (19%)
  other arithmetic  56.7 us (10%)
  local copies, waits for them, and re-layouts  43 us (8%)
  starting transfers between devices  22.1 us (4%)
  between operations  14.2 us (3%)
    unnamed x2, waiting for transfers between devices  267 us
    dot_general x16, matrix products, reverse_step(): jnp.dot(pre_grad, recur_weight.T, precision=lax.Precision.HIGHEST, prefer...  71.7 us
    mul x16, other arithmetic, reverse_step(): return ((new_rec, cell_total * forget), pre_grad)  24.4 us
    ppermute x4, waiting for transfers between devices, passed_along(): return lax.ppermute(shard, axis, pairs)  21.5 us
    squeeze x16, local copies, waits for them, and re-layouts, cell_backward(): lax.scan(reverse_step, begin, (gate_vals, cell_vals, prev_cells, out_grad...  15 us
    ppermute x4, starting transfers between devices, passed_along(): return lax.ppermute(shard, axis, pairs)  13.4 us
    mul x16, other arithmetic, reverse_step(): cell_total * candidate * in_gate * (1.0 - in_gate)  13.2 us
    all_to_all x1, waiting for transfers between devices, local(): lax.all_to_all(conv_in_grad.astype(jnp.bfloat16), 'snap', split_axis=0, c...  11.8 us
  transfers between devices with their start and end apart: 6, of which 5 were waited for; matrix products, arithmetic and copies ran while one was open for 5% of the time, Pallas kernels for 0%

commit v1 on v0

--- a/solution.py
+++ b/solution.py
@@ -73,6 +73,18 @@
     tile_values,
     tile_mask,
 ):
+
+    def convert_ends(local_x, axis_key, along_dim, array_axis):
+        return jnp.concatenate(
+            jax.lax.all_to_all(
+                jnp.stack(jnp.split(local_x, jax.lax.axis_size(axis_key), axis=along_dim), axis=0),
+                axis_name=axis_key,
+                split_axis=0,
+                concat_axis=0,
+            ),
+            axis=array_axis,
+        )
+
     pre_grads, prev_hidden = cell_backward(saved_gates, saved_cells, out_grad, recur_weight)
     conv_in_grad = jnp.einsum(
         "tvg,fg->tvf",
@@ -99,8 +111,8 @@
         lax.psum_scatter(input_term, ("snap", "vert"), scatter_dimension=0, tiled=True),
         lax.psum_scatter(recur_term, ("snap", "vert"), scatter_dimension=0, tiled=True),
     )
-    rounded = lax.all_to_all(
-        conv_in_grad.astype(jnp.bfloat16), "snap", split_axis=0, concat_axis=1, tiled=True
+    rounded = convert_ends(
+        conv_in_grad.astype(jnp.bfloat16), axis_key="snap", along_dim=0, array_axis=1
     )
     tiles = tile_values[:, 0]
     partial_value = jnp.einsum("skij,sif->skjf", tiles, rounded, preferred_element_type=jnp.float32)

time: 542 us -> 551 us (1.017)
  local copies, waits for them, and re-layouts: 43 us -> 52.8 us
    unnamed x17 -> x32, local copies, waits for them, and re-layouts: 5.98 us -> 15.1 us
where the time goes in v1:
time: 551 us; the launch traced here: 547 us
  waiting for transfers between devices  300 us (54%)
  matrix products  102 us (19%)
  other arithmetic  56.7 us (10%)
  local copies, waits for them, and re-layouts  52.8 us (10%)
  starting transfers between devices  22.2 us (4%)
  between operations  14.2 us (3%)
    unnamed x2, waiting for transfers between devices  267 us
    dot_general x16, matrix products, reverse_step(): jnp.dot(pre_grad, recur_weight.T, precision=lax.Precision.HIGHEST, prefer...  71.7 us
    mul x16, other arithmetic, reverse_step(): return ((new_rec, cell_total * forget), pre_grad)  24.4 us
    ppermute x4, waiting for transfers between devices, passed_along(): return lax.ppermute(shard, axis, pairs)  21.3 us
    unnamed x32, local copies, waits for them, and re-layouts  15.1 us
    squeeze x16, local copies, waits for them, and re-layouts, cell_backward(): lax.scan(reverse_step, begin, (gate_vals, cell_vals, prev_cells, out_grad...  15 us
    ppermute x4, starting transfers between devices, passed_along(): return lax.ppermute(shard, axis, pairs)  13.6 us
    mul x16, other arithmetic, reverse_step(): cell_total * candidate * in_gate * (1.0 - in_gate)  13.2 us
  transfers between devices with their start and end apart: 6, of which 5 were waited for; matrix products, arithmetic and copies ran while one was open for 5% of the time, Pallas kernels for 0%

profile of v1, /device:TPU:8, one launch (start us, length us, event | category | flops | bytes accessed | tf_op | source)
XLA Modules:
  0.0 547.4 jit_solution(3144443936734232795)
XLA Ops:
  7.2 1.2 slice.74
  8.4 2.0 convert_element_type.19
  10.4 3.5 convert_element_type.18
  14.8 2.1 broadcast_in_dim.15
  17.5 135.6 %while.19 = (s32[]{:T(128)}, f32[32,384]{1,0:T(8,128)}, f32[32,384]{1,0:T(8,128)}, f32[16,32,1536]{2,1,0:T(8,128)}, f32[16,32,384]{2,1,0:T(8,128)}, /*index=5*/f...) while((s32[]{:T(128)}, f32[32,384]{1,0:T(8,128)}, ...), condition=%wide.region_1.2_spmd.clone, body=%wide.region_0.1_spmd.clone.sunk | while | flops 227082240 | bytes 4227227 | solution.py:51
  18.4 1.5 slice_multiply_fusion.2
  21.5 4.5 fusion.44
  26.9 1.5 slice_multiply_fusion.2
  29.9 4.5 fusion.44
  35.4 1.5 slice_multiply_fusion.2
  38.4 4.5 fusion.44
  43.8 1.5 slice_multiply_fusion.2
  46.9 4.5 fusion.44
  52.3 1.5 slice_multiply_fusion.2
  55.3 4.5 fusion.44
  60.8 1.5 slice_multiply_fusion.2
  63.8 4.5 fusion.44
  69.2 1.5 slice_multiply_fusion.2
  72.3 4.5 fusion.44
  77.7 1.5 slice_multiply_fusion.2
  80.8 4.5 fusion.44
  86.2 1.5 slice_multiply_fusion.2
  89.3 4.5 fusion.44
  94.7 1.5 slice_multiply_fusion.2
  97.8 4.5 fusion.44
  103.2 1.5 slice_multiply_fusion.2
  106.2 4.5 fusion.44
  111.7 1.5 slice_multiply_fusion.2
  114.7 4.5 fusion.44
  120.2 1.5 slice_multiply_fusion.2
  123.2 4.5 fusion.44
  128.6 1.5 slice_multiply_fusion.2
  131.7 4.5 fusion.44
  137.1 1.5 slice_multiply_fusion.2
  140.2 4.5 fusion.44
  145.6 1.5 slice_multiply_fusion.2
  148.6 4.5 fusion.44
  153.1 7.8 %fusion.15 = bf16[16,32,384]{2,1,0:T(8,128)(2,1)S(1)} fusion(f32[16,32,1536]{2,1,0:T(8,128)} %get-tuple-element.183, f32[384,1536]{1,0:T(8,128)} %param.16), kind=kOutput, calls=%fused_computation.28 | convolution fusion | flops 3624075264 | bytes 5898240 | tf_op jit(solution)/shard_map/tvg,fg->tvf/dot_general | solution.py:89
  170.7 8.6 %all-to-all-start = ((bf16[16,1,32,384]{3,2,1,0:T(8,128)(2,1)}), bf16[16,1,32,384]{3,2,1,0:T(8,128)(2,1)}, u32[]{:S(2)}, u32[]{:S(2)}) async-start(bf16[16,1,32,384]{3,2,1,0:T(8,128)(2,1)} %constant_dynamic-update-slice_fusion), calls=%async_computation | async-start | bytes 786432 | tf_op jit(solution)/shard_map/all_to_all | solution.py:79
  179.3 1.9 slice.80
  181.3 11.8 %all-to-all-done = bf16[16,1,32,384]{3,2,1,0:T(8,128)(2,1)} async-done(((bf16[16,1,32,384]{3,2,1,0:T(8,128)(2,1)}), bf16[16,1,32,384]{3,2,1,0:T(8,128)(2,1)}, u32[]{:S(2)}, u32[]{:S(2)}) %all-to-all-start) | async-done | bytes 393248 | tf_op jit(solution)/shard_map/all_to_all | solution.py:79
  193.0 2.2 multiply_bitcast_fusion
  195.3 1.7 slice_bitcast_fusion.3
  197.0 1.8 copy-done.1
  198.8 4.9 collective-permute-start
  203.7 3.1 collective-permute-start.1
  206.8 2.8 collective-permute-start.2
  209.6 2.8 collective-permute-start.3
  212.4 5.4 convolution_bitcast_fusion
  217.8 3.2 reshape.68
  221.0 7.7 %convolution_bitcast_fusion.1 = f32[384,1536]{0,1:T(8,128)} fusion(f32[16,32,1536]{2,1,0:T(8,128)} %get-tuple-element.183, f32[16,32,384]{2,1,0:T(8,128)S(1)} %copy-done.5), kind=kOutput, calls=%fused_computation.22 | convolution fusion | flops 3623878656 | bytes 6291456 | tf_op jit(solution)/shard_map/tvf,tvg->fg/dot_general | solution.py:96
  228.7 3.1 copy.20
  231.9 3.1 reshape.67
  235.0 4.6 collective-permute-done.1
  240.0 16.3 %collective-permute-done.3 = f32[1,512,384]{1,2,0:T(8,128)} collective-permute-done((f32[1,512,384]{1,2,0:T(8,128)}, f32[1,512,384]{1,2,0:T(8,128)}, u32[]{:S(2)}, u32[]{:S(2)}) %collective-permute-start.3) | collective-permute-done | bytes 786464 | tf_op jit(solution)/shard_map/ppermute | solution.py:10
  256.4 2.5 fusion.22
  258.9 2.2 convolution_bitcast_fusion.3
  261.1 2.1 copy.19
  263.2 1.9 reshape.66
  265.2 4.6 convolution_bitcast_fusion.2
  269.8 266.6 %all-reduce.8.cloned.1.call-done = (f32[147456]{0:T(1024)}, f32[589824]{0:T(1024)}, f32[589824]{0:T(1024)}) async-done(((f32[147456]{0:T(1024)}, f32[589824]{0:T(1024)}, f32[589824]{0:T(1024)}), (f32[147456]{0:T(1024)}, f32[589824]{0:T(1024)}, f32[589824]{0:T(1024)})) %all-reduce.8.cloned.1.call-update) | async-done | bytes 5308432
  536.4 1.4 dynamic-slice.1
  537.8 1.4 dynamic-slice.2
  539.2 1.4 dynamic-slice
  (85 shorter events, 51.3 us)
Async XLA Ops:
  7.2 185.9 %copy-start = (bf16[1,1,5,512,512]{4,3,2,1,0:T(8,128)(2,1)S(1)}, bf16[1,1,5,512,512]{4,3,2,1,0:T(8,128)(2,1)}, u32[]{:S(2)}) copy-start(bf16[1,1,5,512,512]{4,3,2,1,0:T(8,128)(2,1)} %param.20) | copy-start | bytes 7864324
  153.1 28.2 %copy-start.6 = (s32[1,1,5]{2,1,0:T(1,128)S(1)}, s32[1,1,5]{2,1,0:T(1,128)}, u32[]{:S(2)}) copy-start(s32[1,1,5]{2,1,0:T(1,128)} %param.21) | copy-start | bytes 64
  170.7 22.4 %all-to-all-start = ((bf16[16,1,32,384]{3,2,1,0:T(8,128)(2,1)}), bf16[16,1,32,384]{3,2,1,0:T(8,128)(2,1)}, u32[]{:S(2)}, u32[]{:S(2)}) async-start(bf16[16,1,32,384]{3,2,1,0:T(8,128)(2,1)} %constant_dynamic-update-slice_fusion), calls=%async_computation | async-start | bytes 786432 | tf_op jit(solution)/shard_map/all_to_all | solution.py:79
  179.3 357.1 %all-reduce.8.cloned.1.call-start = ((), (), s32[]{:S(2)}) async-start(), calls=%async_computation.1 | async-start | bytes 10616832
  195.2 3.5 copy-start.1
  195.3 17.1 %copy-start.2 = (f32[16,32,1536]{2,1,0:T(8,128)S(1)}, f32[16,32,1536]{2,1,0:T(8,128)}, u32[]{:S(2)}) copy-start(f32[16,32,1536]{2,1,0:T(8,128)} %get-tuple-element.183) | copy-start | bytes 9437188
  195.3 17.1 %copy-start.4 = (f32[15,32,384]{2,1,0:T(8,128)S(1)}, f32[15,32,384]{2,1,0:T(8,128)}, u32[]{:S(2)}) copy-start(f32[15,32,384]{2,1,0:T(8,128)} %slice.80) | copy-start | bytes 2211844
  198.8 36.2 %collective-permute-start = (f32[1,512,384]{1,2,0:T(8,128)}, f32[1,512,384]{1,2,0:T(8,128)}, u32[]{:S(2)}, u32[]{:S(2)}) collective-permute-start(f32[1,512,384]{1,2,0:T(8,128)} %get-tuple-element.241), channel_id=1, source_target_pairs={{2,0},{3,1},{4,2},{5,3},{6,4},{7,5},{8,6},{9,7},{10,8},{11,9},{12,... | collective-permute-start | bytes 2359304 | tf_op jit(solution)/shard_map/ppermute | solution.py:10
  203.7 35.9 %collective-permute-start.1 = (f32[1,512,384]{1,2,0:T(8,128)}, f32[1,512,384]{1,2,0:T(8,128)}, u32[]{:S(2)}, u32[]{:S(2)}) collective-permute-start(f32[1,512,384]{1,2,0:T(8,128)} %get-tuple-element.244), channel_id=1, source_target_pairs={{1,0},{2,1},{3,2},{4,3},{5,4},{6,5},{7,6},{8,7},{9,8},{10,9},{11,1... | collective-permute-start | bytes 2359304 | tf_op jit(solution)/shard_map/ppermute | solution.py:10
  206.8 33.2 %collective-permute-start.2 = (f32[1,512,384]{1,2,0:T(8,128)}, f32[1,512,384]{1,2,0:T(8,128)}, u32[]{:S(2)}, u32[]{:S(2)}) collective-permute-start(f32[1,512,384]{1,2,0:T(8,128)} %get-tuple-element.243), channel_id=1, source_target_pairs={{0,1},{1,2},{2,3},{3,4},{4,5},{5,6},{6,7},{7,8},{8,9},{9,10},{10,1... | collective-permute-start | bytes 2359304 | tf_op jit(solution)/shard_map/ppermute | solution.py:10
  209.6 46.8 %collective-permute-start.3 = (f32[1,512,384]{1,2,0:T(8,128)}, f32[1,512,384]{1,2,0:T(8,128)}, u32[]{:S(2)}, u32[]{:S(2)}) collective-permute-start(f32[1,512,384]{1,2,0:T(8,128)} %get-tuple-element.242), channel_id=1, source_target_pairs={{0,2},{1,3},{2,4},{3,5},{4,6},{5,7},{6,8},{7,9},{8,10},{9,11},{10,... | collective-permute-start | bytes 2359304 | tf_op jit(solution)/shard_map/ppermute | solution.py:10
  217.8 3.2 copy-start.5
  235.0 23.9 %copy-start.3 = (f32[1,512,384]{2,1,0:T(8,128)S(1)}, f32[1,512,384]{2,1,0:T(8,128)}, u32[]{:S(2)}) copy-start(f32[1,512,384]{2,1,0:T(8,128)} %param.19) | copy-start | bytes 2359300
Sparse Core Ops, SparseCore 0:
  265.3 271.0 all-reduce.7
